TPU v7x, 32 devices: a whole 2x2x4 slice. The times are simulated.
32 devices in a mesh: op: 4 (over y, x), str: 8 (over z, core).
Axes of the slice: x: 2, y: 2, z: 4, core: 2. Of those that a mesh axis runs over, the one named last changes fastest.
Arguments:
- coeffs: float32 [4096, 4096], P('str'), may hold values from -6 to 6
- previous: float32 [4096, 4096], P('str'), may hold values from -6 to 6
- block_values: bfloat16 [4, 32, 6, 128, 128], P('op'), may hold values from -0.21875 to 0.21875
- block_cols: int32 [4, 32, 6], P('op'), may hold values from 0 to 31, as said below
Outputs:
- advanced: float32 [4096, 4096], P('str')
Inputs may be any that keep to these rules, and one draw needn't show every extreme that they name: For every term k and block row r, block_cols[k, r, 0] equals r and the 6 entries of block_cols[k, r] are distinct.
All inputs are finite; a program needn't handle non-finite values.
Results may differ from a plain program's by a relative error of at most 0.0003.
Values sent between devices are 32-bit elements; how exact they have to be, the bound alone decides.
A program may use at most 192 MiB of HBM per device.

v0:
```python
import math
import jax
import jax.numpy as jnp
from jax import lax
from jax.sharding import PartitionSpec as P

STEPS = 2


def per_device(coeffs, previous, block_values, block_cols):
    local_terms = block_values.shape[0]
    step_scale = 2.0 / math.sqrt(local_terms * lax.axis_size("op"))
    factors = block_values.astype(jnp.float32)
    row_count, full_width = coeffs.shape
    block_size = block_values.shape[-1]
    block_count = full_width // block_size
    slot_count = block_cols.shape[2]
    regrouped = lax.all_to_all(
        previous.reshape(row_count, block_count, block_size),
        "str",
        split_axis=1,
        concat_axis=0,
        tiled=True,
    )
    earlier = regrouped.reshape(full_width, row_count).T
    current = coeffs
    for step_index in range(STEPS):
        column_list = block_cols[0].reshape(-1)
        term_factors = factors[0]
        gathered = jnp.take(
            current.reshape(row_count, block_count, block_size), column_list, axis=1
        )
        gathered = gathered.reshape(row_count, block_count, slot_count, block_size)
        beta_side = jnp.einsum(
            "arjc,rjoc->aro", gathered, term_factors, precision=lax.Precision.HIGHEST
        )
        received = lax.all_to_all(beta_side, "str", split_axis=1, concat_axis=0, tiled=True)
        group_count = received.shape[1]
        item_count = received.shape[2]
        grouped = jnp.take(
            received.reshape(block_count, block_size, group_count, item_count), column_list, axis=0
        )
        grouped = grouped.reshape(block_count, slot_count, block_size, group_count, item_count)
        result = jnp.einsum(
            "rjoc,rjcnm->nmro", term_factors, grouped, precision=lax.Precision.HIGHEST
        )
        moved = result.reshape(group_count, item_count, full_width)
        summed = moved.reshape(row_count, full_width)
        updated = step_scale * lax.psum(summed, "op") - earlier
        earlier, current = (current, updated)
    return current


def solution(mesh):
    placed = (P("str", None), P("str", None), P("op", None, None, None, None), P("op", None, None))
    return jax.shard_map(
        per_device, mesh=mesh, in_specs=placed, out_specs=P("str", None), check_vma=False
    )
```

profile of v0, /device:TPU:0, one launch (start us, length us, event | category | flops | bytes accessed | tf_op | source)
XLA Modules:
  0.0 1236.2 jit_solution(6269851794979325475)
XLA Ops:
  6.5 0.8 copy.25
  7.3 0.1 reshape_squeeze.4
  7.4 9.0 copy.26
  16.4 9.0 copy.27
  25.3 22.2 %gather_fusion = f32[192,512,128]{2,1,0:T(8,128)} fusion(f32[512,32,128]{2,0,1:T(8,128)} %copy.27, s32[1024]{0:T(1024)S(1)} %pad_clamp_fusion), kind=kCustom, calls=%fused_computation.clone | custom fusion | bytes 100664064 | tf_op jit(solution)/shard_map/jit(_take)/gather | solution.py:30
  47.6 34.0 %broadcast_select_fusion.3 = f32[192,512,128]{2,1,0:T(8,128)} fusion(f32[192,512,128]{2,1,0:T(8,128)} %gather_fusion, pred[192]{0:T(512)(128)(4,1)S(1)} %compare_and_fusion), kind=kLoop, calls=%fused_computation.7 | loop fusion | flops 12582912 | bytes 100663488 | tf_op jit(solution)/shard_map/jit(_take)/select_n | solution.py:30
  81.6 30.1 %fusion.8 = f32[512,32,128]{2,0,1:T(8,128)} fusion(f32[512,32,6,128]{3,0,2,1:T(8,128)} %bitcast.92, bf16[1,32,6,128,128]{4,3,2,1,0:T(8,128)(2,1)} %param.10), kind=kOutput, calls=%fused_computation.19 | convolution fusion | flops 19327352832 | bytes 65011712 | tf_op jit(solution)/shard_map/arjc,rjoc->aro/dot_general | solution.py:34
  111.7 6.4 all-to-all-start
  118.1 9.0 copy.31
  127.1 175.0 %all-to-all-done = f32[512,32,128]{2,0,1:T(8,128)} async-done(((f32[512,32,128]{2,0,1:T(8,128)}), f32[512,32,128]{2,0,1:T(8,128)}, u32[]{:S(2)}, u32[]{:S(2)}) %all-to-all-start) | async-done | bytes 8388640 | tf_op jit(solution)/shard_map/all_to_all | solution.py:37
  302.1 4.9 all-to-all-start.1
  307.0 0.0 all-reduce.3.cloned.1.call-start
  307.1 7.7 copy.28
  314.7 22.2 %gather_fusion.1 = f32[192,128,4,128]{3,1,2,0:T(8,128)} fusion(f32[32,128,4,128]{3,1,0,2:T(8,128)} %bitcast.91, s32[1024]{0:T(1024)S(1)} %pad_clamp_fusion), kind=kCustom, calls=%fused_computation.1.clone | custom fusion | bytes 100664064 | tf_op jit(solution)/shard_map/jit(_take)/gather | solution.py:40
  337.0 34.9 %broadcast_select_fusion.1 = f32[192,128,4,128]{3,1,2,0:T(8,128)} fusion(f32[192,128,4,128]{3,1,2,0:T(8,128)} %gather_fusion.1, pred[192]{0:T(512)(128)(4,1)S(1)} %compare_and_fusion), kind=kLoop, calls=%fused_computation.5 | loop fusion | flops 12582912 | bytes 100663488 | tf_op jit(solution)/shard_map/jit(_take)/select_n | solution.py:40
  371.9 48.2 %fusion.14 = f32[4,128,32,128]{3,1,0,2:T(8,128)} fusion(f32[32,6,128,4,128]{4,2,3,1,0:T(8,128)} %bitcast.95, bf16[1,32,6,128,128]{4,3,2,1,0:T(8,128)(2,1)} %param.10), kind=kOutput, calls=%fused_computation.21 | convolution fusion | flops 19327352832 | bytes 65011712 | tf_op jit(solution)/shard_map/rjoc,rjcnm->nmro/dot_general | solution.py:44
  420.1 8.2 copy.30
  428.4 11.7 copy.55
  440.1 0.0 all-reduce.3.cloned.1.call-update
  440.1 0.0 all-reduce.5.cloned.1.call-start
  440.1 50.7 %all-to-all-done.1 = f32[512,32,128]{0,2,1:T(8,128)} async-done(((f32[512,32,128]{0,2,1:T(8,128)}), f32[512,32,128]{0,2,1:T(8,128)}, u32[]{:S(2)}, u32[]{:S(2)}) %all-to-all-start.1) | async-done | bytes 8388640 | tf_op jit(solution)/shard_map/all_to_all | solution.py:18
  490.9 8.4 copy.33
  499.2 11.7 copy.50
  511.0 102.6 %all-reduce.3.cloned.1.call-done = f32[512,4096]{1,0:T(8,128)} async-done(((f32[512,4096]{1,0:T(8,128)}), f32[512,4096]{1,0:T(8,128)}) %all-reduce.3.cloned.1.call-update) | async-done | bytes 8388624 | tf_op jit(solution)/shard_map/psum | solution.py:49
  613.6 11.3 bitcast_subtract_fusion
  624.9 9.0 copy.34
  633.9 8.9 copy.35
  642.8 22.2 %gather_fusion.2 = f32[192,512,128]{2,1,0:T(8,128)} fusion(f32[512,32,128]{2,0,1:T(8,128)} %copy.35, s32[1024]{0:T(1024)S(1)} %pad_clamp_fusion), kind=kCustom, calls=%fused_computation.2.clone | custom fusion | bytes 100664064 | tf_op jit(solution)/shard_map/jit(_take)/gather | solution.py:30
  665.0 34.0 %broadcast_select_fusion.2 = f32[192,512,128]{2,1,0:T(8,128)} fusion(f32[192,512,128]{2,1,0:T(8,128)} %gather_fusion.2, pred[192]{0:T(512)(128)(4,1)S(1)} %compare_and_fusion), kind=kLoop, calls=%fused_computation.6 | loop fusion | flops 12582912 | bytes 100663488 | tf_op jit(solution)/shard_map/jit(_take)/select_n | solution.py:30
  699.1 30.1 %fusion.11 = f32[512,32,128]{2,0,1:T(8,128)} fusion(f32[512,32,6,128]{3,0,2,1:T(8,128)} %bitcast.93, bf16[1,32,6,128,128]{4,3,2,1,0:T(8,128)(2,1)} %param.10), kind=kOutput, calls=%fused_computation.20 | convolution fusion | flops 19327352832 | bytes 65011712 | tf_op jit(solution)/shard_map/arjc,rjoc->aro/dot_general | solution.py:34
  729.2 188.9 %all_to_all.45 = f32[512,32,128]{2,0,1:T(8,128)S(1)} all-to-all(f32[512,32,128]{2,0,1:T(8,128)} %fusion.11), channel_id=1, replica_groups=mesh['op'=4,'str'=8] {'str'}, dimensions={1} | all-to-all | bytes 16777216 | tf_op jit(solution)/shard_map/all_to_all | solution.py:37
  918.1 4.0 copy.36
  922.1 22.2 %gather_fusion.3 = f32[192,128,4,128]{3,1,2,0:T(8,128)} fusion(f32[32,128,4,128]{3,1,0,2:T(8,128)} %bitcast.90, s32[1024]{0:T(1024)S(1)} %pad_clamp_fusion), kind=kCustom, calls=%fused_computation.3.clone | custom fusion | bytes 100664064 | tf_op jit(solution)/shard_map/jit(_take)/gather | solution.py:40
  944.3 34.9 %broadcast_select_fusion = f32[192,128,4,128]{3,1,2,0:T(8,128)} fusion(f32[192,128,4,128]{3,1,2,0:T(8,128)} %gather_fusion.3, pred[192]{0:T(512)(128)(4,1)S(1)} %compare_and_fusion), kind=kLoop, calls=%fused_computation.4 | loop fusion | flops 12582912 | bytes 100663488 | tf_op jit(solution)/shard_map/jit(_take)/select_n | solution.py:40
  979.3 47.8 %fusion.17 = f32[4,128,32,128]{3,1,0,2:T(8,128)} fusion(f32[32,6,128,4,128]{4,2,3,1,0:T(8,128)} %bitcast.94, bf16[1,32,6,128,128]{4,3,2,1,0:T(8,128)(2,1)} %param.10), kind=kOutput, calls=%fused_computation.22 | convolution fusion | flops 19327352832 | bytes 65011712 | tf_op jit(solution)/shard_map/rjoc,rjcnm->nmro/dot_general | solution.py:44
  1027.1 8.2 copy.38
  1035.4 11.8 copy.54
  1047.1 0.0 all-reduce.5.cloned.1.call-update
  1047.1 170.5 %all-reduce.5.cloned.1.call-done = f32[512,4096]{1,0:T(8,128)} async-done(((f32[512,4096]{1,0:T(8,128)}), f32[512,4096]{1,0:T(8,128)}) %all-reduce.5.cloned.1.call-update) | async-done | bytes 8388624 | tf_op jit(solution)/shard_map/psum | solution.py:49
  1217.6 11.3 sub.7
  (3 shorter events, 0.0 us)
Async XLA Ops:
  111.7 190.3 %all-to-all-start = ((f32[512,32,128]{2,0,1:T(8,128)}), f32[512,32,128]{2,0,1:T(8,128)}, u32[]{:S(2)}, u32[]{:S(2)}) async-start(f32[512,32,128]{2,0,1:T(8,128)} %fusion.8), calls=%async_computation | async-start | bytes 16777216 | tf_op jit(solution)/shard_map/all_to_all | solution.py:37
  302.1 188.8 %all-to-all-start.1 = ((f32[512,32,128]{0,2,1:T(8,128)}), f32[512,32,128]{0,2,1:T(8,128)}, u32[]{:S(2)}, u32[]{:S(2)}) async-start(f32[512,32,128]{0,2,1:T(8,128)} %bitcast.97), calls=%async_computation.1 | async-start | bytes 16777216 | tf_op jit(solution)/shard_map/all_to_all | solution.py:18
  307.0 306.5 %all-reduce.3.cloned.1.call-start = ((), (), s32[]{:S(2)}) async-start(), calls=%async_computation.3 | async-start | bytes 16777216 | tf_op jit(solution)/shard_map/psum | solution.py:49
  440.1 777.5 %all-reduce.5.cloned.1.call-start = ((), (), s32[]{:S(2)}) async-start(), calls=%async_computation.4 | async-start | bytes 16777216 | tf_op jit(solution)/shard_map/psum | solution.py:49
Sparse Core Ops, SparseCore 0:
  440.2 173.3 all-reduce.2
  1047.3 170.2 all-reduce.4
where the time goes:
time: 1250 us; the launch traced here: 1240 us
  waiting for transfers between devices  499 us (40%)
  local copies, waits for them, and re-layouts  206 us (16%)
  blocking collectives  189 us (15%)
  other arithmetic  161 us (13%)
  matrix products  156 us (12%)
  between operations  13.9 us (1%)
    psum x2, waiting for transfers between devices, per_device(): updated = step_scale * lax.psum(summed, 'op') - earlier  273 us
    all_to_all x1, blocking collectives, per_device(): lax.all_to_all(beta_side, 'str', split_axis=1, concat_axis=0, tiled=True)  189 us
    all_to_all x1, waiting for transfers between devices, per_device(): lax.all_to_all(beta_side, 'str', split_axis=1, concat_axis=0, tiled=True)  175 us
    dot_general x2, matrix products, per_device(): jnp.einsum('rjoc,rjcnm->nmro', term_factors, grouped, precision=lax.Preci...  96.1 us
    select_n x3, other arithmetic, per_device(): jnp.take(received.reshape(block_count, block_size, group_count, item_coun...  69.9 us
    select_n x2, other arithmetic, per_device(): jnp.take(current.reshape(row_count, block_count, block_size), column_list...  68.1 us
    dot_general x2, matrix products, per_device(): jnp.einsum('arjc,rjoc->aro', gathered, term_factors, precision=lax.Precis...  60.2 us
    unnamed x6, local copies, waits for them, and re-layouts  53.9 us
  transfers between devices with their start and end apart: 4, of which 4 were waited for; matrix products, arithmetic and copies ran while one was open for 13% of the time, Pallas kernels for 0%

commit v1 on v0

--- a/solution.py
+++ b/solution.py
@@ -5,6 +5,22 @@
 from jax.sharding import PartitionSpec as P
 
 STEPS = 2
+
+
+def settle_the_digits(mine_x, join_dim, mat):
+    even = mine_x.shape
+    last = mine_x.reshape(*even[:join_dim], mat, even[join_dim] // mat, *even[join_dim + 1 :])
+    piece_next = jnp.moveaxis(last, join_dim, 0)
+    return piece_next
+
+
+def change_sample(inputs, dim_i):
+    inputs = jnp.moveaxis(inputs, 0, dim_i)
+    mid_arr = inputs.shape
+    lower = inputs.reshape(
+        *mid_arr[:dim_i], mid_arr[dim_i] * mid_arr[dim_i + 1], *mid_arr[dim_i + 2 :]
+    )
+    return lower
 
 
 def per_device(coeffs, previous, block_values, block_cols):
@@ -15,12 +31,26 @@
     block_size = block_values.shape[-1]
     block_count = full_width // block_size
     slot_count = block_cols.shape[2]
-    regrouped = lax.all_to_all(
-        previous.reshape(row_count, block_count, block_size),
-        "str",
-        split_axis=1,
-        concat_axis=0,
-        tiled=True,
+
+    def switch_the_slot(inp, net_axis, frame_in, frame):
+        everything, part_next = (lax.axis_size(net_axis), lax.axis_index(net_axis))
+        wide_out = settle_the_digits(inp, frame_in, everything)
+        made = [wide_out[part_next]]
+        for s in tuple(range(1, everything)):
+            block_out = wide_out[(part_next + s) % everything]
+            kept_arr = lax.ppermute(
+                block_out,
+                net_axis,
+                [(dev_i, (dev_i + s) % everything) for dev_i in range(everything)],
+            )
+            made.append(kept_arr)
+        carry_in = jnp.stack(made, 0)
+        wide_out = carry_in[(part_next - jnp.arange(everything)) % everything]
+        carry_out = change_sample(wide_out, frame)
+        return carry_out
+
+    regrouped = switch_the_slot(
+        previous.reshape(row_count, block_count, block_size), "str", 1, frame=0
     )
     earlier = regrouped.reshape(full_width, row_count).T
     current = coeffs

time: 1250 us -> 1300 us (1.040)
  blocking collectives: 189 us -> 425 us
  waiting for transfers between devices: 499 us -> 273 us
  local copies, waits for them, and re-layouts: 206 us -> 231 us
  starting transfers between devices: 11.4 us -> 25.1 us
    all_to_all x1 -> x2, blocking collectives: 189 us -> 425 us  [per_device(): lax.all_to_all(beta_side, 'str', split_axis=1, concat_axis=0, tiled=True)]
    all_to_all x2 -> x0, waiting for transfers between devices: 226 us -> none  [the longest x1 175 us: per_device(): lax.all_to_all(beta_side, 'str', split_axis=1, concat_axis=0, tiled=True)]
    psum x2, waiting for transfers between devices: 273 us -> 171 us  [per_device(): updated = step_scale * lax.psum(summed, 'op') - earlier]
    ppermute x0 -> x7, waiting for transfers between devices: none -> 102 us  [switch_the_slot(): lax.ppermute(block_out, net_axis, [(dev_i, (dev_i + s) % everything) for...]
    ppermute x0 -> x7, starting transfers between devices: none -> 25 us  [switch_the_slot(): lax.ppermute(block_out, net_axis, [(dev_i, (dev_i + s) % everything) for...]
    gather x0 -> x2, local copies, waits for them, and re-layouts: none -> 18.3 us  [switch_the_slot(): wide_out = carry_in[(part_next - jnp.arange(everything)) % everything]]
    another operation x0 -> x3, local copies, waits for them, and re-layouts: none -> 16.5 us  [the longest x1 10.9 us: settle_the_digits(): mine_x.reshape(*even[:join_dim], mat, even[join_dim] // mat, *even[join_d...]
    unnamed x6 -> x19, local copies, waits for them, and re-layouts: 53.9 us -> 55.8 us
  transfers between devices with their start and end apart: 4 -> 9, of which waited for: 4 -> 5; matrix products, arithmetic and copies ran while one was open for 13% -> 4% of each run, Pallas kernels for 0% -> 0%
where the time goes in v1:
time: 1300 us; the launch traced here: 1290 us
  blocking collectives  425 us (33%)
  waiting for transfers between devices  273 us (21%)
  local copies, waits for them, and re-layouts  231 us (18%)
  other arithmetic  161 us (12%)
  matrix products  157 us (12%)
  starting transfers between devices  25.1 us (2%)
  between operations  14.1 us (1%)
    all_to_all x2, blocking collectives, per_device(): lax.all_to_all(beta_side, 'str', split_axis=1, concat_axis=0, tiled=True)  425 us
    psum x2, waiting for transfers between devices, per_device(): updated = step_scale * lax.psum(summed, 'op') - earlier  171 us
    ppermute x7, waiting for transfers between devices, switch_the_slot(): lax.ppermute(block_out, net_axis, [(dev_i, (dev_i + s) % everything) for...  102 us
    dot_general x2, matrix products, per_device(): jnp.einsum('rjoc,rjcnm->nmro', term_factors, grouped, precision=lax.Preci...  96.3 us
    select_n x3, other arithmetic, per_device(): jnp.take(received.reshape(block_count, block_size, group_count, item_coun...  69.9 us
    select_n x2, other arithmetic, per_device(): jnp.take(current.reshape(row_count, block_count, block_size), column_list...  68.1 us
    dot_general x2, matrix products, per_device(): jnp.einsum('arjc,rjoc->aro', gathered, term_factors, precision=lax.Precis...  60.2 us
    unnamed x19, local copies, waits for them, and re-layouts  55.8 us
  transfers between devices with their start and end apart: 9, of which 5 were waited for; matrix products, arithmetic and copies ran while one was open for 4% of the time, Pallas kernels for 0%

profile of v1, /device:TPU:0, one launch (start us, length us, event | category | flops | bytes accessed | tf_op | source)
XLA Modules:
  0.0 1286.1 jit_solution(16999478889715099370)
XLA Ops:
  6.5 0.8 copy.32
  7.4 9.0 copy.33
  16.4 8.9 copy.34
  25.3 22.2 %gather_fusion.1 = f32[192,512,128]{2,1,0:T(8,128)} fusion(f32[512,32,128]{2,0,1:T(8,128)} %copy.34, s32[1024]{0:T(1024)S(1)} %pad_clamp_fusion.1), kind=kCustom, calls=%fused_computation.clone | custom fusion | bytes 100664064 | tf_op jit(solution)/shard_map/jit(_take)/gather | solution.py:60
  47.6 34.1 %broadcast_select_fusion.3 = f32[192,512,128]{2,1,0:T(8,128)} fusion(f32[192,512,128]{2,1,0:T(8,128)} %gather_fusion.1, pred[192]{0:T(512)(128)(4,1)S(1)} %compare_and_fusion), kind=kLoop, calls=%fused_computation.8 | loop fusion | flops 12582912 | bytes 100663488 | tf_op jit(solution)/shard_map/jit(_take)/select_n | solution.py:60
  81.6 30.1 %fusion.8 = f32[512,32,128]{2,0,1:T(8,128)} fusion(f32[512,32,6,128]{3,0,2,1:T(8,128)} %bitcast.129, bf16[1,32,6,128,128]{4,3,2,1,0:T(8,128)(2,1)} %param.10), kind=kOutput, calls=%fused_computation.20 | convolution fusion | flops 19327352832 | bytes 65011712 | tf_op jit(solution)/shard_map/arjc,rjoc->aro/dot_general | solution.py:64
  111.7 190.2 %all_to_all.30 = f32[512,32,128]{2,0,1:T(8,128)S(1)} all-to-all(f32[512,32,128]{2,0,1:T(8,128)} %fusion.8), channel_id=1, replica_groups=mesh['op'=4,'str'=8] {'str'}, dimensions={1} | all-to-all | bytes 16777216 | tf_op jit(solution)/shard_map/all_to_all | solution.py:67
  302.0 4.0 copy.35
  305.9 22.2 %gather_fusion.2 = f32[192,128,4,128]{3,1,2,0:T(8,128)} fusion(f32[32,128,4,128]{3,1,0,2:T(8,128)} %bitcast.128, s32[1024]{0:T(1024)S(1)} %pad_clamp_fusion.1), kind=kCustom, calls=%fused_computation.1.clone | custom fusion | bytes 100664064 | tf_op jit(solution)/shard_map/jit(_take)/gather | solution.py:70
  328.2 34.9 %broadcast_select_fusion.1 = f32[192,128,4,128]{3,1,2,0:T(8,128)} fusion(f32[192,128,4,128]{3,1,2,0:T(8,128)} %gather_fusion.2, pred[192]{0:T(512)(128)(4,1)S(1)} %compare_and_fusion), kind=kLoop, calls=%fused_computation.6 | loop fusion | flops 12582912 | bytes 100663488 | tf_op jit(solution)/shard_map/jit(_take)/select_n | solution.py:70
  363.1 48.3 %fusion.14 = f32[4,128,32,128]{3,1,0,2:T(8,128)} fusion(f32[32,6,128,4,128]{4,2,3,1,0:T(8,128)} %bitcast.132, bf16[1,32,6,128,128]{4,3,2,1,0:T(8,128)(2,1)} %param.10), kind=kOutput, calls=%fused_computation.22 | convolution fusion | flops 19327352832 | bytes 65011712 | tf_op jit(solution)/shard_map/rjoc,rjcnm->nmro/dot_general | solution.py:74
  411.4 8.2 copy.37
  419.7 11.7 copy.85
  431.5 10.9 reshape_reshape.13
  442.4 4.5 constant_dynamic-slice_fusion
  447.3 1.7 collective-permute-start.2
  449.1 2.5 collective-permute-start.3
  451.9 1.0 fusion.20
  453.0 20.8 %collective-permute-done = f32[512,4,128]{2,0,1:T(8,128)S(1)} collective-permute-done((f32[512,4,128]{2,0,1:T(8,128)S(1)}, f32[512,4,128]{2,0,1:T(8,128)S(1)}, u32[]{:S(2)}, u32[]{:S(2)}) %collective-permute-start) | collective-permute-done | bytes 1048608 | tf_op jit(solution)/shard_map/ppermute | solution.py:41
  473.8 1.1 bitcast_dynamic-update-slice_fusion.6
  474.9 0.3 collective-permute-done.1
  475.2 20.6 %collective-permute-start.6 = (f32[512,4,128]{2,0,1:T(8,128)S(1)}, f32[512,4,128]{2,0,1:T(8,128)S(1)}, u32[]{:S(2)}, u32[]{:S(2)}) collective-permute-start(f32[512,4,128]{2,0,1:T(8,128)S(1)} %bitcast.143), channel_id=1, source_target_pairs={{0,7},{1,0},{2,1},{3,2},{4,3},{5,4},{6,5},{7,6},{8,15},{9,8},{10,9... | collective-permute-start | bytes 3145736 | tf_op jit(solution)/shard_map/ppermute | solution.py:41
  495.8 1.1 bitcast_dynamic-update-slice_fusion.5
  496.8 67.3 %collective-permute-done.2 = f32[512,4,128]{2,0,1:T(8,128)S(1)} collective-permute-done((f32[512,4,128]{2,0,1:T(8,128)S(1)}, f32[512,4,128]{2,0,1:T(8,128)S(1)}, u32[]{:S(2)}, u32[]{:S(2)}) %collective-permute-start.2) | collective-permute-done | bytes 1048608 | tf_op jit(solution)/shard_map/ppermute | solution.py:41
  564.1 1.1 bitcast_dynamic-update-slice_fusion.4
  565.2 1.0 bitcast_dynamic-update-slice_fusion.3
  566.2 1.1 bitcast_dynamic-update-slice_fusion.2
  567.3 1.1 bitcast_dynamic-update-slice_fusion.1
  568.4 13.9 %collective-permute-done.6 = f32[512,4,128]{2,0,1:T(8,128)S(1)} collective-permute-done((f32[512,4,128]{2,0,1:T(8,128)S(1)}, f32[512,4,128]{2,0,1:T(8,128)S(1)}, u32[]{:S(2)}, u32[]{:S(2)}) %collective-permute-start.6) | collective-permute-done | bytes 1048608 | tf_op jit(solution)/shard_map/ppermute | solution.py:41
  582.3 1.1 bitcast_dynamic-update-slice_fusion
  583.4 8.0 gather_fusion
  591.4 10.3 copy.46
  601.7 14.7 %copy.70 = f32[64,8,8,512]{3,1,2,0:T(8,128)} copy(f32[64,8,8,512]{3,2,1,0:T(8,128)} %bitcast.138) | data formatting | bytes 16777216
  616.4 11.3 bitcast_subtract_fusion
  627.7 9.0 copy.47
  636.7 8.9 copy.48
  645.7 22.7 %gather_fusion.3 = f32[192,512,128]{2,1,0:T(8,128)} fusion(f32[512,32,128]{2,0,1:T(8,128)} %copy.48, s32[1024]{0:T(1024)S(1)} %pad_clamp_fusion.1), kind=kCustom, calls=%fused_computation.2.clone | custom fusion | bytes 100664064 | tf_op jit(solution)/shard_map/jit(_take)/gather | solution.py:60
  668.3 34.1 %broadcast_select_fusion.2 = f32[192,512,128]{2,1,0:T(8,128)} fusion(f32[192,512,128]{2,1,0:T(8,128)} %gather_fusion.3, pred[192]{0:T(512)(128)(4,1)S(1)} %compare_and_fusion), kind=kLoop, calls=%fused_computation.7 | loop fusion | flops 12582912 | bytes 100663488 | tf_op jit(solution)/shard_map/jit(_take)/select_n | solution.py:60
  702.4 30.1 %fusion.11 = f32[512,32,128]{2,0,1:T(8,128)} fusion(f32[512,32,6,128]{3,0,2,1:T(8,128)} %bitcast.130, bf16[1,32,6,128,128]{4,3,2,1,0:T(8,128)(2,1)} %param.10), kind=kOutput, calls=%fused_computation.21 | convolution fusion | flops 19327352832 | bytes 65011712 | tf_op jit(solution)/shard_map/arjc,rjoc->aro/dot_general | solution.py:64
  732.5 235.1 %all_to_all.31 = f32[512,32,128]{2,0,1:T(8,128)S(1)} all-to-all(f32[512,32,128]{2,0,1:T(8,128)} %fusion.11), channel_id=1, replica_groups=mesh['op'=4,'str'=8] {'str'}, dimensions={1} | all-to-all | bytes 16777216 | tf_op jit(solution)/shard_map/all_to_all | solution.py:67
  967.6 4.0 copy.49
  971.6 22.2 %gather_fusion.4 = f32[192,128,4,128]{3,1,2,0:T(8,128)} fusion(f32[32,128,4,128]{3,1,0,2:T(8,128)} %bitcast.127, s32[1024]{0:T(1024)S(1)} %pad_clamp_fusion.1), kind=kCustom, calls=%fused_computation.3.clone | custom fusion | bytes 100664064 | tf_op jit(solution)/shard_map/jit(_take)/gather | solution.py:70
  993.8 34.9 %broadcast_select_fusion = f32[192,128,4,128]{3,1,2,0:T(8,128)} fusion(f32[192,128,4,128]{3,1,2,0:T(8,128)} %gather_fusion.4, pred[192]{0:T(512)(128)(4,1)S(1)} %compare_and_fusion), kind=kLoop, calls=%fused_computation.5 | loop fusion | flops 12582912 | bytes 100663488 | tf_op jit(solution)/shard_map/jit(_take)/select_n | solution.py:70
  1028.8 48.0 %fusion.17 = f32[4,128,32,128]{3,1,0,2:T(8,128)} fusion(f32[32,6,128,4,128]{4,2,3,1,0:T(8,128)} %bitcast.131, bf16[1,32,6,128,128]{4,3,2,1,0:T(8,128)(2,1)} %param.10), kind=kOutput, calls=%fused_computation.23 | convolution fusion | flops 19327352832 | bytes 65011712 | tf_op jit(solution)/shard_map/rjoc,rjcnm->nmro/dot_general | solution.py:74
  1076.8 8.2 copy.51
  1085.0 11.8 copy.84
  1096.8 170.7 %all-reduce.5.cloned.1.call-done = f32[512,4096]{1,0:T(8,128)} async-done(((f32[512,4096]{1,0:T(8,128)}), f32[512,4096]{1,0:T(8,128)}) %all-reduce.5.cloned.1.call-update) | async-done | bytes 8388624 | tf_op jit(solution)/shard_map/psum | solution.py:79
  1267.5 11.3 sub.22
  (25 shorter events, 1.0 us)
Async XLA Ops:
  6.5 609.9 %all-reduce.3.cloned.1.call-start = ((), (), s32[]{:S(2)}) async-start(), calls=%async_computation.2 | async-start | bytes 16777216 | tf_op jit(solution)/shard_map/psum | solution.py:79
  431.4 836.1 %all-reduce.5.cloned.1.call-start = ((), (), s32[]{:S(2)}) async-start(), calls=%async_computation.3 | async-start | bytes 16777216 | tf_op jit(solution)/shard_map/psum | solution.py:79
  447.0 26.8 %collective-permute-start = (f32[512,4,128]{2,0,1:T(8,128)S(1)}, f32[512,4,128]{2,0,1:T(8,128)S(1)}, u32[]{:S(2)}, u32[]{:S(2)}) collective-permute-start(f32[512,4,128]{2,0,1:T(8,128)S(1)} %bitcast.149), channel_id=1, source_target_pairs={{0,1},{1,2},{2,3},{3,4},{4,5},{5,6},{6,7},{7,0},{8,9},{9,10},{10,1... | collective-permute-start | bytes 3145736 | tf_op jit(solution)/shard_map/ppermute | solution.py:41
  447.1 28.1 %collective-permute-start.1 = (f32[512,4,128]{2,0,1:T(8,128)S(1)}, f32[512,4,128]{2,0,1:T(8,128)S(1)}, u32[]{:S(2)}, u32[]{:S(2)}) collective-permute-start(f32[512,4,128]{2,0,1:T(8,128)S(1)} %bitcast.148), channel_id=1, source_target_pairs={{0,2},{1,3},{2,4},{3,5},{4,6},{5,7},{6,0},{7,1},{8,10},{9,11},{10,... | collective-permute-start | bytes 3145736 | tf_op jit(solution)/shard_map/ppermute | solution.py:41
  447.3 116.8 %collective-permute-start.2 = (f32[512,4,128]{2,0,1:T(8,128)S(1)}, f32[512,4,128]{2,0,1:T(8,128)S(1)}, u32[]{:S(2)}, u32[]{:S(2)}) collective-permute-start(f32[512,4,128]{2,0,1:T(8,128)S(1)} %bitcast.147), channel_id=1, source_target_pairs={{0,3},{1,4},{2,5},{3,6},{4,7},{5,0},{6,1},{7,2},{8,11},{9,12},{10,... | collective-permute-start | bytes 3145736 | tf_op jit(solution)/shard_map/ppermute | solution.py:41
  449.1 116.1 %collective-permute-start.3 = (f32[512,4,128]{2,0,1:T(8,128)S(1)}, f32[512,4,128]{2,0,1:T(8,128)S(1)}, u32[]{:S(2)}, u32[]{:S(2)}) collective-permute-start(f32[512,4,128]{2,0,1:T(8,128)S(1)} %bitcast.146), channel_id=1, source_target_pairs={{0,4},{1,5},{2,6},{3,7},{4,0},{5,1},{6,2},{7,3},{8,12},{9,13},{10,... | collective-permute-start | bytes 3145736 | tf_op jit(solution)/shard_map/ppermute | solution.py:41
  451.6 114.6 %collective-permute-start.4 = (f32[512,4,128]{2,0,1:T(8,128)S(1)}, f32[512,4,128]{2,0,1:T(8,128)S(1)}, u32[]{:S(2)}, u32[]{:S(2)}) collective-permute-start(f32[512,4,128]{2,0,1:T(8,128)S(1)} %bitcast.145), channel_id=1, source_target_pairs={{0,5},{1,6},{2,7},{3,0},{4,1},{5,2},{6,3},{7,4},{8,13},{9,14},{10,... | collective-permute-start | bytes 3145736 | tf_op jit(solution)/shard_map/ppermute | solution.py:41
  473.8 93.5 %collective-permute-start.5 = (f32[512,4,128]{2,0,1:T(8,128)S(1)}, f32[512,4,128]{2,0,1:T(8,128)S(1)}, u32[]{:S(2)}, u32[]{:S(2)}) collective-permute-start(f32[512,4,128]{2,0,1:T(8,128)S(1)} %bitcast.144), channel_id=1, source_target_pairs={{0,6},{1,7},{2,0},{3,1},{4,2},{5,3},{6,4},{7,5},{8,14},{9,15},{10,... | collective-permute-start | bytes 3145736 | tf_op jit(solution)/shard_map/ppermute | solution.py:41
  475.2 107.1 %collective-permute-start.6 = (f32[512,4,128]{2,0,1:T(8,128)S(1)}, f32[512,4,128]{2,0,1:T(8,128)S(1)}, u32[]{:S(2)}, u32[]{:S(2)}) collective-permute-start(f32[512,4,128]{2,0,1:T(8,128)S(1)} %bitcast.143), channel_id=1, source_target_pairs={{0,7},{1,0},{2,1},{3,2},{4,3},{5,4},{6,5},{7,6},{8,15},{9,8},{10,9... | collective-permute-start | bytes 3145736 | tf_op jit(solution)/shard_map/ppermute | solution.py:41
Sparse Core Ops, SparseCore 0:
  431.5 170.8 all-reduce.2
  1096.9 170.5 all-reduce.4
